TPU v7x, 256 devices: a whole 4x4x8 slice. The times are simulated.
256 devices in a mesh: dp: 16 (over y_hi, x, core), feat: 16 (over y_lo, z).
Axes of the slice: x: 4, y: 4 (y_hi: 2, y_lo: 2; y = y_hi * 2 + y_lo), z: 8, core: 2. Of those that a mesh axis runs over, the one named last changes fastest.
Arguments:
- inputs: float32 [8192, 8192], P('dp', 'feat'), may hold values from -6 to 6
- partner_bits: int32 [16, 4], P('feat'), may hold values from 0 to 3, each once within a row
- block_weights: float32 [16, 512, 5, 512], P('feat', 'dp'), may hold values from -0.125 to 0.125
- low_left: float32 [16, 512, 256], P('feat', 'dp'), may hold values from -0.0625 to 0.0625
- low_right: float32 [16, 256, 512], P('feat', 'dp'), may hold values from -0.375 to 0.375
- cotangent: float32 [8192, 8192], P('dp', 'feat'), may hold values from -6 to 6
Outputs:
- outputs: float32 [8192, 8192], P('dp', 'feat')
- input_grad: float32 [8192, 8192], P('dp', 'feat')
- block_grads: float32 [16, 512, 5, 512], P('feat', 'dp')
- left_grads: float32 [16, 512, 256], P('feat', 'dp')
- right_grads: float32 [16, 256, 512], P('feat', 'dp')
Inputs may be any that keep to these rules, and one draw needn't show every extreme that they name: `partner_bits`: each row holds every bit number 0 .. 3 once.
All inputs are finite; a program needn't handle non-finite values.
Results may differ from a plain program's by a relative error of at most 0.000086.
Values sent between devices are 32-bit elements; how exact they have to be, the bound alone decides.
A program may use at most 128 MiB of HBM per device.

v0:
```python
import math

import jax
import jax.numpy as jnp
from jax import lax
from jax.sharding import Mesh
from jax.sharding import PartitionSpec as P

DP = ("dp_0", "dp_1", "dp_2")


def swapped(block, axis, apart):
    count = lax.axis_size(axis)
    route = []
    for low in range(count):
        high = low | 1 << apart
        if high != low and high < count:
            route += [(low, high), (high, low)]
    return lax.ppermute(block, axis, route)


def joined_along(pieces, dim):
    shape = list(pieces.shape[1:])
    shape[dim] *= pieces.shape[0]
    return jnp.moveaxis(pieces, 0, dim).reshape(shape)


def one_gather(arrays, axis, dims):
    vector = jnp.concatenate([a.reshape(-1) for a in arrays])
    lines, at, finished = (lax.all_gather(vector, axis), 0, [])
    for a, dim in zip(arrays, dims):
        pieces = lines[:, at : at + a.size].reshape(-1, *a.shape)
        finished.append(joined_along(pieces, dim))
        at += a.size
    return tuple(finished)


def cut_along(shard, dim, size):
    shape = shard.shape
    pieces = shard.reshape(*shape[:dim], size, shape[dim] // size, *shape[dim + 1 :])
    return jnp.moveaxis(pieces, dim, 0)


def summed_on_arrival(shard, axis, dim):
    pieces = cut_along(shard, dim, lax.axis_size(axis))
    arrived = lax.all_to_all(pieces, axis, split_axis=0, concat_axis=0, tiled=True)
    return arrived.sum(axis=0)


def filled_up(lines, size):
    spare = -lines.shape[0] % size
    if not spare:
        return lines
    return jnp.concatenate([lines, jnp.zeros((spare, *lines.shape[1:]), lines.dtype)])


def sent_to_all(shard, axis):
    copies = jnp.broadcast_to(shard, (lax.axis_size(axis), *shard.shape))
    return lax.all_to_all(copies, axis, split_axis=0, concat_axis=0, tiled=True)


def collect(shard, axis, dim):
    return joined_along(sent_to_all(shard, axis), dim)


def nested_sum(shard, axes):
    lines = shard.reshape(-1, shard.shape[-1])
    own = summed_on_arrival(filled_up(lines, lax.axis_size(axes)), axes, 0)
    whole = collect(own, axes, 0)
    return whole[: len(lines)].reshape(shard.shape)


def sum_in_two_steps(shard, axes, dim):
    far, near = axes
    pieces = cut_along(shard, dim, lax.axis_size(far))
    nearer = summed_on_arrival(pieces, near, dim + 1)
    arrived = lax.all_to_all(nearer, far, split_axis=0, concat_axis=0, tiled=True)
    return arrived.sum(axis=0)


def in_one_piece(arrays, axis, dim, along):
    columns = [a.reshape(*a.shape[:along], -1) for a in arrays]
    both = jnp.concatenate(columns, axis=along)
    whole, at, finished = (sum_in_two_steps(both, axis, dim), 0, [])
    for a, column in zip(arrays, columns):
        share = whole[..., at : at + column.shape[along]]
        finished.append(share.reshape(*share.shape[:along], *a.shape[along:]))
        at += column.shape[along]
    return tuple(finished)


def on_device(inputs, partner_bits, block_weights, low_left, low_right, cotangent):
    highest = lax.Precision.HIGHEST
    row_count, block = inputs.shape
    sections = partner_bits.shape[1]
    my_bits = partner_bits[0]
    arrived = []
    for level in range(sections):
        arrived.append(swapped(inputs, "feat", level))
    by_bit = jnp.stack(arrived)
    sources = jnp.concatenate([inputs[None], by_bit[my_bits]], axis=0)
    bit_numbers = jnp.arange(sections, dtype=jnp.int32)
    matches = (my_bits[:, None] == bit_numbers[None, :]).astype(jnp.int32)
    slot_of_bit = jnp.sum(matches * bit_numbers[:, None], axis=0)
    left_full, right_full = one_gather((low_left, low_right), DP, (1, 1))
    left_full = left_full[0]
    right_full = right_full[0]
    code_part = jnp.dot(inputs, left_full, precision=highest, preferred_element_type=jnp.float32)
    code_grad_part = jnp.dot(
        cotangent, right_full.T, precision=highest, preferred_element_type=jnp.float32
    )
    codes = nested_sum(code_part, "feat")
    full_weights = lax.all_gather(block_weights, DP, axis=1, tiled=True)[0]
    sparse = jnp.einsum("sri,iso->ro", sources, full_weights, precision=highest)
    outputs = sparse + jnp.dot(
        codes, right_full, precision=highest, preferred_element_type=jnp.float32
    )
    code_grads = nested_sum(code_grad_part, "feat")
    products = jnp.einsum("ro,iso->sri", cotangent, full_weights, precision=highest)
    grad_scale = 1.0 / math.sqrt(row_count * lax.axis_size(DP))
    block_grad = jnp.einsum("sri,ro->iso", sources, cotangent, precision=highest) * grad_scale
    right_grad = (
        jnp.dot(codes.T, cotangent, precision=highest, preferred_element_type=jnp.float32)
        * grad_scale
    )
    left_grad = (
        jnp.dot(inputs.T, code_grads, precision=highest, preferred_element_type=jnp.float32)
        * grad_scale
    )
    input_grad = products[0] + jnp.dot(
        code_grads, left_full.T, precision=highest, preferred_element_type=jnp.float32
    )
    for level in range(sections):
        outgoing = products[1 + slot_of_bit[level]]
        input_grad = input_grad + swapped(outgoing, "feat", level)
    block_grads, left_grads, right_grads = (
        *in_one_piece((block_grad[None], left_grad[None]), (("dp_0", "dp_1"), "dp_2"), 1, 2),
        sum_in_two_steps(right_grad[None], (("dp_0", "dp_1"), "dp_2"), 1),
    )
    return (outputs, input_grad, block_grads, left_grads, right_grads)


def solution(mesh):
    split = Mesh(
        mesh.devices.reshape(2, 4, 2, mesh.shape["feat"]), ("dp_0", "dp_1", "dp_2", "feat")
    )
    in_specs = (
        P(DP, "feat"),
        P("feat", None),
        P("feat", DP, None, None),
        P("feat", DP, None),
        P("feat", DP, None),
        P(DP, "feat"),
    )
    out_specs = (
        P(DP, "feat"),
        P(DP, "feat"),
        P("feat", DP, None, None),
        P("feat", DP, None),
        P("feat", DP, None),
    )
    return jax.shard_map(
        on_device, mesh=split, in_specs=in_specs, out_specs=out_specs, check_vma=False
    )
```

profile of v0, /device:TPU:32, one launch (start us, length us, event | category | flops | bytes accessed | tf_op | source)
XLA Modules:
  0.0 425.8 jit_solution(702935430014383913)
XLA Ops:
  10.3 53.6 %all-gather.6.cloned.1.call-done = f32[262144]{0:T(1024)} async-done(((f32[16384]{0:T(1024)}), f32[262144]{0:T(1024)}) %all-gather.6.cloned.1.call-update) | async-done | bytes 1048592 | tf_op jit(solution)/shard_map/all_gather | solution.py:30
  69.6 7.5 %all-to-all-start.2 = ((f32[16,32,256]{2,1,0:T(8,128)}), f32[16,32,256]{2,1,0:T(8,128)S(1)}, u32[]{:S(2)}, u32[]{:S(2)}) async-start(f32[16,32,256]{2,1,0:T(8,128)} %bitcast.108), calls=%async_computation.2 | async-start | bytes 1048576 | tf_op jit(solution)/shard_map/all_to_all | solution.py:46
  83.0 9.9 %all-to-all-done.2 = f32[16,32,256]{2,1,0:T(8,128)S(1)} async-done(((f32[16,32,256]{2,1,0:T(8,128)}), f32[16,32,256]{2,1,0:T(8,128)S(1)}, u32[]{:S(2)}, u32[]{:S(2)}) %all-to-all-start.2) | async-done | bytes 524320 | tf_op jit(solution)/shard_map/all_to_all | solution.py:46
  93.7 4.9 %all-to-all-start = ((f32[16,32,256]{2,1,0:T(8,128)}), f32[16,32,256]{2,1,0:T(8,128)S(1)}, u32[]{:S(2)}, u32[]{:S(2)}) async-start(f32[16,32,256]{2,1,0:T(8,128)} %bitcast.107), calls=%async_computation | async-start | bytes 1048576 | tf_op jit(solution)/shard_map/all_to_all | solution.py:46
  107.6 6.5 %all-to-all-done = f32[16,32,256]{2,1,0:T(8,128)S(1)} async-done(((f32[16,32,256]{2,1,0:T(8,128)}), f32[16,32,256]{2,1,0:T(8,128)S(1)}, u32[]{:S(2)}, u32[]{:S(2)}) %all-to-all-start) | async-done | bytes 524320 | tf_op jit(solution)/shard_map/all_to_all | solution.py:46
  115.1 18.8 %all-to-all-start.3 = ((f32[16,32,256]{2,1,0:T(8,128)}), f32[16,32,256]{2,1,0:T(8,128)S(1)}, u32[]{:S(2)}, u32[]{:S(2)}) async-start(f32[16,32,256]{2,1,0:T(8,128)} %broadcast_in_dim.15), calls=%async_computation.3 | async-start | bytes 1048576 | tf_op jit(solution)/shard_map/all_to_all | solution.py:59
  133.9 23.9 %collective-permute-done = f32[512,512]{1,0:T(8,128)} collective-permute-done((f32[512,512]{1,0:T(8,128)S(1)}, f32[512,512]{1,0:T(8,128)}, u32[]{:S(2)}, u32[]{:S(2)}) %collective-permute-start) | collective-permute-done | bytes 1048608 | tf_op jit(solution)/shard_map/ppermute | solution.py:19
  157.8 7.7 %collective-permute-done.1 = f32[512,512]{1,0:T(8,128)} collective-permute-done((f32[512,512]{1,0:T(8,128)S(1)}, f32[512,512]{1,0:T(8,128)}, u32[]{:S(2)}, u32[]{:S(2)}) %collective-permute-start.1) | collective-permute-done | bytes 1048608 | tf_op jit(solution)/shard_map/ppermute | solution.py:19
  165.6 22.1 %collective-permute-done.2 = f32[512,512]{1,0:T(8,128)} collective-permute-done((f32[512,512]{1,0:T(8,128)S(1)}, f32[512,512]{1,0:T(8,128)}, u32[]{:S(2)}, u32[]{:S(2)}) %collective-permute-start.2) | collective-permute-done | bytes 1048608 | tf_op jit(solution)/shard_map/ppermute | solution.py:19
  192.3 5.0 %gather_fusion = f32[4,512,512]{2,1,0:T(8,128)} fusion(f32[4,512,512]{2,1,0:T(8,128)} %pad_maximum_fusion.3, s32[1024]{0:T(1024)S(1)} %pad_clamp_fusion), kind=kCustom, calls=%fused_computation | custom fusion | bytes 8388624 | tf_op jit(solution)/shard_map/gather | solution.py:101
  198.4 14.2 %all-to-all-done.3 = f32[16,32,256]{2,1,0:T(8,128)S(1)} async-done(((f32[16,32,256]{2,1,0:T(8,128)}), f32[16,32,256]{2,1,0:T(8,128)S(1)}, u32[]{:S(2)}, u32[]{:S(2)}) %all-to-all-start.3) | async-done | bytes 524320 | tf_op jit(solution)/shard_map/all_to_all | solution.py:59
  213.5 14.2 %all-to-all-start.1 = ((f32[16,32,256]{2,1,0:T(8,128)}), f32[16,32,256]{2,1,0:T(8,128)}, u32[]{:S(2)}, u32[]{:S(2)}) async-start(f32[16,32,256]{2,1,0:T(8,128)} %broadcast_in_dim.14), calls=%async_computation.1 | async-start | bytes 1048576 | tf_op jit(solution)/shard_map/all_to_all | solution.py:59
  227.7 10.5 %multiply_bitcast_fusion = f32[512,5,512]{2,0,1:T(8,128)S(1)} fusion(f32[4,512,512]{2,1,0:T(8,128)} %gather_fusion, f32[1,512,512]{2,1,0:T(8,128)S(1)} %bitcast.102, f32[512,512]{1,0:T(8,128)S(1)} %copy-done), kind=kOutput, calls=%fused_computation.7 | convolution fusion | flops 8055685120 | bytes 11534336 | tf_op jit(solution)/shard_map/sri,ro->iso/dot_general | solution.py:121
  238.2 6.5 %copy.37 = f32[512,5,512]{2,1,0:T(8,128)} copy(f32[512,5,512]{2,0,1:T(8,128)S(1)} %multiply_bitcast_fusion) | data formatting | bytes 10485760 | tf_op jit(solution)/shard_map/mul | solution.py:121
  244.7 8.7 %concatenate.16 = f32[8,1,2,32,2560]{4,3,2,0,1:T(8,128)} reshape(f32[512,5,512]{2,1,0:T(8,128)} %copy.37) | data formatting | bytes 10485760 | tf_op jit(solution)/shard_map/concatenate | solution.py:83
  265.5 4.9 %all_to_all.40 = f32[2,8,1,16,512]{4,3,1,2,0:T(8,128)} all-to-all(f32[2,8,1,16,512]{4,3,1,2,0:T(8,128)S(1)} %bitcast.109), channel_id=1, replica_groups=mesh['dp_0'=2,'dp_1'=4,'dp_2'=2,'feat'=16] {'dp_2'}, dimensions={0} | all-to-all | bytes 1048576 | tf_op jit(solution)/shard_map/all_to_all | solution.py:46
  270.4 6.3 %all-to-all-start.4 = ((f32[2,8,1,32,2816]{4,3,1,2,0:T(8,128)}), f32[2,8,1,32,2816]{4,3,1,2,0:T(8,128)}, u32[]{:S(2)}, u32[]{:S(2)}) async-start(f32[2,8,1,32,2816]{4,3,1,2,0:T(8,128)} %copy.39), calls=%async_computation.4 | async-start | bytes 11534336 | tf_op jit(solution)/shard_map/all_to_all | solution.py:46
  282.3 5.0 %all-to-all-start.7 = ((f32[8,1,16,512]{3,2,1,0:T(8,128)}), f32[8,1,16,512]{3,2,1,0:T(8,128)S(1)}, u32[]{:S(2)}, u32[]{:S(2)}) async-start(f32[8,1,16,512]{3,2,1,0:T(8,128)} %bitcast.114), calls=%async_computation.7 | async-start | bytes 524288 | tf_op jit(solution)/shard_map/all_to_all | solution.py:77
  287.4 5.0 %reduce_sum.74 = f32[8,32,2816]{2,1,0:T(8,128)} reduce(f32[2,8,1,32,2816]{4,3,1,2,0:T(8,128)} %all-to-all-done.4, f32[]{:T(128)} %constant.24.clone.1), dimensions={0,2}, to_apply=%region_3.0 | reduce | flops 720896 | bytes 8650756 | tf_op jit(solution)/shard_map/reduce_sum | solution.py:47
  306.8 10.4 %fusion = f32[512,5,512]{2,0,1:T(8,128)S(1)} fusion(f32[1,512,5,512]{3,1,2,0:T(8,128)} %all-gather.4.cloned.1.call-done, f32[512,512]{1,0:T(8,128)S(1)} %copy-done), kind=kOutput, calls=%fused_computation.3 | convolution fusion | flops 8053063680 | bytes 11534336 | tf_op jit(solution)/shard_map/ro,iso->sri/dot_general | solution.py:119
  332.7 4.9 %all-to-all-done.5 = f32[8,1,32,2816]{3,2,1,0:T(8,128)} async-done(((f32[8,1,32,2816]{3,2,1,0:T(8,128)}), f32[8,1,32,2816]{3,2,1,0:T(8,128)}, u32[]{:S(2)}, u32[]{:S(2)}) %all-to-all-start.5) | async-done | bytes 2883616 | tf_op jit(solution)/shard_map/all_to_all | solution.py:77
  341.0 12.4 %fusion.12 = f32[512,512]{1,0:T(8,128)} fusion(f32[512,512]{1,0:T(8,128)} %fusion.23, f32[1,512,5,512]{3,1,2,0:T(8,128)} %all-gather.4.cloned.1.call-done, f32[4,512,512]{2,1,0:T(8,128)} %gather_fusion, f32[1,512,512]{2,1,0:T(8,128)S(1)} %bitcast.103), kind=kOutput, calls=%fused_computation.16 | convolution fusion | flops 8054636544 | bytes 12582912 | tf_op jit(solution)/shard_map/sri,iso->ro/dot_general | solution.py:114
  353.4 15.5 %collective-permute-done.4 = f32[512,512]{0,1:T(8,128)} collective-permute-done((f32[512,512]{0,1:T(8,128)}, f32[512,512]{0,1:T(8,128)}, u32[]{:S(2)}, u32[]{:S(2)}) %collective-permute-start.4) | collective-permute-done | bytes 1048608 | tf_op jit(solution)/shard_map/ppermute | solution.py:19
  368.9 45.0 %collective-permute-done.5 = f32[512,512]{0,1:T(8,128)} collective-permute-done((f32[512,512]{0,1:T(8,128)}, f32[512,512]{0,1:T(8,128)}, u32[]{:S(2)}, u32[]{:S(2)}) %collective-permute-start.5) | collective-permute-done | bytes 1048608 | tf_op jit(solution)/shard_map/ppermute | solution.py:19
  (72 shorter events, 82.8 us)
Async XLA Ops:
  7.2 60.3 %copy-start = (f32[512,512]{1,0:T(8,128)S(1)}, f32[512,512]{1,0:T(8,128)}, u32[]{:S(2)}) copy-start(f32[512,512]{1,0:T(8,128)} %param.11) | copy-start | bytes 3145732
  7.2 56.7 %all-gather.6.cloned.1.call-start = ((), (), s32[]{:S(2)}) async-start(), calls=%async_computation.9 | async-start | bytes 1114112 | tf_op jit(solution)/shard_map/all_gather | solution.py:30
  9.5 297.2 %all-gather.4.cloned.1.call-start = ((), (), s32[]{:S(2)}) async-start(), calls=%async_computation.8 | async-start | bytes 5570560 | tf_op jit(solution)/shard_map/all_gather | solution.py:113
  10.3 68.0 %copy-start.2 = (f32[512,512]{1,0:T(8,128)S(1)}, f32[512,512]{1,0:T(8,128)}, u32[]{:S(2)}) copy-start(f32[512,512]{1,0:T(8,128)} %param.6) | copy-start | bytes 3145732
  67.5 9.6 %copy-start.3 = (f32[256,512]{1,0:T(8,128)}, f32[256,512]{1,0:T(8,128)S(1)}, u32[]{:S(2)}) copy-start(f32[256,512]{1,0:T(8,128)S(1)} %squeeze_reshape_transpose_reshape.7) | copy-start | bytes 1572868
  68.6 65.3 %copy-start.7 = (s32[1,4]{1,0:T(1,128)S(1)}, s32[1,4]{1,0:T(1,128)}, u32[]{:S(2)}) copy-start(s32[1,4]{1,0:T(1,128)} %param.7) | copy-start | bytes 52
  69.6 23.3 %all-to-all-start.2 = ((f32[16,32,256]{2,1,0:T(8,128)}), f32[16,32,256]{2,1,0:T(8,128)S(1)}, u32[]{:S(2)}, u32[]{:S(2)}) async-start(f32[16,32,256]{2,1,0:T(8,128)} %bitcast.108), calls=%async_computation.2 | async-start | bytes 1048576 | tf_op jit(solution)/shard_map/all_to_all | solution.py:46
  93.7 20.4 %all-to-all-start = ((f32[16,32,256]{2,1,0:T(8,128)}), f32[16,32,256]{2,1,0:T(8,128)S(1)}, u32[]{:S(2)}, u32[]{:S(2)}) async-start(f32[16,32,256]{2,1,0:T(8,128)} %bitcast.107), calls=%async_computation | async-start | bytes 1048576 | tf_op jit(solution)/shard_map/all_to_all | solution.py:46
  98.6 59.3 %collective-permute-start = (f32[512,512]{1,0:T(8,128)S(1)}, f32[512,512]{1,0:T(8,128)}, u32[]{:S(2)}, u32[]{:S(2)}) collective-permute-start(f32[512,512]{1,0:T(8,128)S(1)} %copy-done.2), channel_id=1, source_target_pairs={{0,1},{1,0},{2,3},{3,2},{4,5},{5,4},{6,7},{7,6},{8,9},{9,8},{10,11... | collective-permute-start | bytes 3145736 | tf_op jit(solution)/shard_map/ppermute | solution.py:19
  98.7 66.8 %collective-permute-start.1 = (f32[512,512]{1,0:T(8,128)S(1)}, f32[512,512]{1,0:T(8,128)}, u32[]{:S(2)}, u32[]{:S(2)}) collective-permute-start(f32[512,512]{1,0:T(8,128)S(1)} %copy-done.2), channel_id=1, source_target_pairs={{0,2},{2,0},{1,3},{3,1},{4,6},{6,4},{5,7},{7,5},{8,10},{10,8},{9,1... | collective-permute-start | bytes 3145736 | tf_op jit(solution)/shard_map/ppermute | solution.py:19
  101.5 86.1 %collective-permute-start.2 = (f32[512,512]{1,0:T(8,128)S(1)}, f32[512,512]{1,0:T(8,128)}, u32[]{:S(2)}, u32[]{:S(2)}) collective-permute-start(f32[512,512]{1,0:T(8,128)S(1)} %copy-done.2), channel_id=1, source_target_pairs={{0,4},{4,0},{1,5},{5,1},{2,6},{6,2},{3,7},{7,3},{8,12},{12,8},{9,1... | collective-permute-start | bytes 3145736 | tf_op jit(solution)/shard_map/ppermute | solution.py:19
  105.1 82.6 %collective-permute-start.3 = (f32[512,512]{1,0:T(8,128)S(1)}, f32[512,512]{1,0:T(8,128)}, u32[]{:S(2)}, u32[]{:S(2)}) collective-permute-start(f32[512,512]{1,0:T(8,128)S(1)} %copy-done.2), channel_id=1, source_target_pairs={{0,8},{8,0},{1,9},{9,1},{2,10},{10,2},{3,11},{11,3},{4,12},{12,4},... | collective-permute-start | bytes 3145736 | tf_op jit(solution)/shard_map/ppermute | solution.py:19
  114.1 1.0 copy-start.5
  115.1 97.5 %all-to-all-start.3 = ((f32[16,32,256]{2,1,0:T(8,128)}), f32[16,32,256]{2,1,0:T(8,128)S(1)}, u32[]{:S(2)}, u32[]{:S(2)}) async-start(f32[16,32,256]{2,1,0:T(8,128)} %broadcast_in_dim.15), calls=%async_computation.3 | async-start | bytes 1048576 | tf_op jit(solution)/shard_map/all_to_all | solution.py:59
  213.5 49.9 %all-to-all-start.1 = ((f32[16,32,256]{2,1,0:T(8,128)}), f32[16,32,256]{2,1,0:T(8,128)}, u32[]{:S(2)}, u32[]{:S(2)}) async-start(f32[16,32,256]{2,1,0:T(8,128)} %broadcast_in_dim.14), calls=%async_computation.1 | async-start | bytes 1048576 | tf_op jit(solution)/shard_map/all_to_all | solution.py:59
  270.4 11.9 %all-to-all-start.4 = ((f32[2,8,1,32,2816]{4,3,1,2,0:T(8,128)}), f32[2,8,1,32,2816]{4,3,1,2,0:T(8,128)}, u32[]{:S(2)}, u32[]{:S(2)}) async-start(f32[2,8,1,32,2816]{4,3,1,2,0:T(8,128)} %copy.39), calls=%async_computation.4 | async-start | bytes 11534336 | tf_op jit(solution)/shard_map/all_to_all | solution.py:46
  282.3 14.1 %all-to-all-start.7 = ((f32[8,1,16,512]{3,2,1,0:T(8,128)}), f32[8,1,16,512]{3,2,1,0:T(8,128)S(1)}, u32[]{:S(2)}, u32[]{:S(2)}) async-start(f32[8,1,16,512]{3,2,1,0:T(8,128)} %bitcast.114), calls=%async_computation.7 | async-start | bytes 524288 | tf_op jit(solution)/shard_map/all_to_all | solution.py:77
  296.4 41.1 %all-to-all-start.5 = ((f32[8,1,32,2816]{3,2,1,0:T(8,128)}), f32[8,1,32,2816]{3,2,1,0:T(8,128)}, u32[]{:S(2)}, u32[]{:S(2)}) async-start(f32[8,1,32,2816]{3,2,1,0:T(8,128)} %bitcast.101), calls=%async_computation.5 | async-start | bytes 5767168 | tf_op jit(solution)/shard_map/all_to_all | solution.py:77
  317.2 2.3 copy-start.1
  319.5 9.6 %copy-start.4 = (f32[256,512]{1,0:T(8,128)S(1)}, f32[256,512]{1,0:T(8,128)}, u32[]{:S(2)}) copy-start(f32[256,512]{1,0:T(8,128)} %copy-done.3) | copy-start | bytes 1572868
  321.6 47.2 %collective-permute-start.4 = (f32[512,512]{0,1:T(8,128)}, f32[512,512]{0,1:T(8,128)}, u32[]{:S(2)}, u32[]{:S(2)}) collective-permute-start(f32[512,512]{0,1:T(8,128)} %get-tuple-element.25), channel_id=1, source_target_pairs={{0,1},{1,0},{2,3},{3,2},{4,5},{5,4},{6,7},{7,6},{8,9},{9,8},{10,11... | collective-permute-start | bytes 3145736 | tf_op jit(solution)/shard_map/ppermute | solution.py:19
  322.1 91.8 %collective-permute-start.5 = (f32[512,512]{0,1:T(8,128)}, f32[512,512]{0,1:T(8,128)}, u32[]{:S(2)}, u32[]{:S(2)}) collective-permute-start(f32[512,512]{0,1:T(8,128)} %get-tuple-element.28), channel_id=1, source_target_pairs={{0,2},{2,0},{1,3},{3,1},{4,6},{6,4},{5,7},{7,5},{8,10},{10,8},{9,1... | collective-permute-start | bytes 3145736 | tf_op jit(solution)/shard_map/ppermute | solution.py:19
  324.5 89.3 %collective-permute-start.6 = (f32[512,512]{0,1:T(8,128)}, f32[512,512]{0,1:T(8,128)}, u32[]{:S(2)}, u32[]{:S(2)}) collective-permute-start(f32[512,512]{0,1:T(8,128)} %get-tuple-element.27), channel_id=1, source_target_pairs={{0,4},{4,0},{1,5},{5,1},{2,6},{6,2},{3,7},{7,3},{8,12},{12,8},{9,1... | collective-permute-start | bytes 3145736 | tf_op jit(solution)/shard_map/ppermute | solution.py:19
  328.1 85.8 %collective-permute-start.7 = (f32[512,512]{0,1:T(8,128)}, f32[512,512]{0,1:T(8,128)}, u32[]{:S(2)}, u32[]{:S(2)}) collective-permute-start(f32[512,512]{0,1:T(8,128)} %get-tuple-element.26), channel_id=1, source_target_pairs={{0,8},{8,0},{1,9},{9,1},{2,10},{10,2},{3,11},{11,3},{4,12},{12,4},... | collective-permute-start | bytes 3145736 | tf_op jit(solution)/shard_map/ppermute | solution.py:19
  (1 other events, 0.8 us)
Sparse Core Ops, SparseCore 0:
  11.3 52.5 all-gather.5
  66.7 84.0 all-gather.3
where the time goes:
time: 432 us; the launch traced here: 426 us
  waiting for transfers between devices  212 us (49%)
  starting transfers between devices  76.7 us (18%)
  matrix products  47.7 us (11%)
  local copies, waits for them, and re-layouts  44.9 us (10%)
  other arithmetic  20.1 us (5%)
  between operations  19.4 us (4%)
  blocking collectives  4.91 us (1%)
    ppermute x8, waiting for transfers between devices, swapped(): return lax.ppermute(block, axis, route)  114 us
    all_gather x1, waiting for transfers between devices, one_gather(): lines, at, finished = (lax.all_gather(vector, axis), 0, [])  53.6 us
    all_to_all x2, starting transfers between devices, sent_to_all(): return lax.all_to_all(copies, axis, split_axis=0, concat_axis=0, tiled=True)  33 us
    all_to_all x3, waiting for transfers between devices, summed_on_arrival(): lax.all_to_all(pieces, axis, split_axis=0, concat_axis=0, tiled=True)  20.2 us
    all_to_all x3, starting transfers between devices, summed_on_arrival(): lax.all_to_all(pieces, axis, split_axis=0, concat_axis=0, tiled=True)  18.7 us
    ppermute x8, starting transfers between devices, swapped(): return lax.ppermute(block, axis, route)  15.4 us
    all_to_all x2, waiting for transfers between devices, sent_to_all(): return lax.all_to_all(copies, axis, split_axis=0, concat_axis=0, tiled=True)  14.2 us
    dot_general x1, matrix products, on_device(): sparse = jnp.einsum('sri,iso->ro', sources, full_weights, precision=highest)  12.4 us
  transfers between devices with their start and end apart: 17, of which 12 were waited for; matrix products, arithmetic and copies ran while one was open for 24% of the time, Pallas kernels for 0%

commit v1 on v0

v1 whole, which is shorter than its diff:
```python
import functools
import math

import jax
import jax.numpy as jnp
from jax import lax
from jax.experimental import pallas as pl
from jax.experimental.pallas import tpu as pltpu
from jax.sharding import PartitionSpec as P

F32, BF16 = jnp.float32, jnp.bfloat16
N = 512
CHUNKS = 8
ROWS = N // CHUNKS
TILE = 128


def dot(a, b, da, db):
    return lax.dot_general(a, b, (((da,), (db,)), ((), ())), preferred_element_type=F32)


def halves(v):
    high = v.astype(BF16)
    return high, (v - high.astype(F32)).astype(BF16)


def product(a, b, da, db):
    (ah, al), (bh, bl) = a, b
    return dot(ah, bh, da, db) + (dot(ah, bl, da, db) + dot(al, bh, da, db))


def kernel(
    x_ref, g_ref, w_ref, l_ref, r_ref,
    out_ref, dx_ref, bg_ref, lr_out_ref,
    lrg, wg, wh, wl, gh, gl, xr,
    cp, cy, cs, cr, cf,
    pb, r4, r2, rf1, rf2, rf3,
    d, er, e, fr, fs, hr,
    load_sem,
    lr_s, lr_r, w_s, w_r,
    x1_s, x2_s, x8_s, f0_s, f1_s, x_r, x8_r,
    cy_s, cy_r, cs_s, cs_r, cg_s, cg_r, ch_s, ch_r,
    p4_s, p2_s, p1_s, p8_s, r4_r, r2_r, rf1_r, rf2_r, rf3_r,
    d_s, d_r, e_s, e_r, h_s, h_r,
):
    dp, f = lax.axis_index("dp"), lax.axis_index("feat")
    b0, b1, b2, b3 = f % 2, (f // 2) % 2, (f // 4) % 2, f // 8
    z = f % 8
    fx1 = f + 1 - 2 * b0
    fx2 = f + 2 - 4 * b1
    fx3 = fx1 + 2 - 4 * b1
    fx6 = fx2 + 4 - 8 * b2
    fx8 = f + 8 - 16 * b3
    odd = (b0 + b1) % 2 == 1
    even = (b0 + b1) % 2 == 0
    core, x, yh = dp % 2, (dp // 2) % 4, dp // 8
    sib = dp + 1 - 2 * core
    far = dp + 8 - 16 * yh

    def at_x(k):
        return (x + k) % 4

    def dp_x(k):
        return yh * 8 + at_x(k) * 2 + core

    def far_x(k):
        return (1 - yh) * 8 + at_x(k) * 2 + core

    def zs(k):
        return (z + k) % 8

    def copy(src, dst, send, recv, to_dp=None, to_f=None):
        return pltpu.make_async_remote_copy(
            src_ref=src,
            dst_ref=dst,
            send_sem=send,
            recv_sem=recv,
            device_id=(dp if to_dp is None else to_dp, f if to_f is None else to_f),
            device_id_type=pl.DeviceIdType.MESH,
        )

    def arrived(dst, recv):
        copy(dst, dst, recv, recv, to_f=fx1).wait_recv()

    lr = lrg.at[dp]
    loads = [
        pltpu.make_async_copy(l_ref, lr.at[pl.ds(0, 32)], load_sem.at[0]),
        pltpu.make_async_copy(r_ref.at[:, pl.ds(0, 256)], lr.at[pl.ds(32, 16)], load_sem.at[1]),
        pltpu.make_async_copy(r_ref.at[:, pl.ds(256, 256)], lr.at[pl.ds(48, 16)], load_sem.at[2]),
        pltpu.make_async_copy(w_ref, wg.at[dp], load_sem.at[3]),
    ]
    for load in loads:
        load.start()

    barrier = pltpu.get_barrier_semaphore()
    peers = [(dp, b3 * 8 + zs(k)) for k in range(1, 8)] + [(dp, fx8)]
    peers += [(sib, f), (far, f)] + [(dp_x(k), f) for k in range(1, 4)]
    for peer in peers:
        pl.semaphore_signal(barrier, inc=1, device_id=peer, device_id_type=pl.DeviceIdType.MESH)
    pl.semaphore_wait(barrier, len(peers))
    for load in loads:
        load.wait()

    def gather(whole, send, recv):
        def put(slot, index, to):
            return copy(whole.at[slot], whole.at[slot], send.at[index], recv.at[slot], to_dp=to)

        first = [put(dp, 0, far)]
        first += [put(dp, k, dp_x(k)) for k in (1, 3, 2)] + [put(dp, 4, sib)]
        second = [put(far, 4 + k, dp_x(k)) for k in (1, 3, 2)] + [put(far, 8, sib)]
        third = [(dp_x(k), put(dp_x(k), 8 + k, sib)) for k in (1, 3, 2)]
        fourth = [(far_x(k), put(far_x(k), 11 + k, sib)) for k in (1, 3, 2)]

        def start():
            for c in first:
                c.start()

        def relay():
            arrived(whole.at[far], recv.at[far])
            for c in second:
                c.start()

        def pass_on(items):
            for slot, c in items:
                arrived(whole.at[slot], recv.at[slot])
                c.start()

        def finish():
            for y in range(2):
                for k in range(4):
                    slot = y * 8 + k * 2 + 1 - core
                    arrived(whole.at[slot], recv.at[slot])

        def drain():
            for c in first + second + [c for _, c in third + fourth]:
                c.wait_send()

        return start, relay, lambda: pass_on(third), lambda: pass_on(fourth), finish, drain

    lr_start, lr_relay, lr_third, lr_fourth, lr_finish, lr_drain = gather(lrg, lr_s, lr_r)
    w_start, w_relay, w_third, w_fourth, w_finish, w_drain = gather(wg, w_s, w_r)

    def rows(c):
        return pl.ds(c * ROWS, ROWS)

    x_to_1 = [
        copy(x_ref.at[rows(c)], xr.at[0, rows(c)], x1_s.at[c], x_r.at[0, c], to_f=fx1)
        for c in range(CHUNKS)
    ]
    x_to_2 = [
        copy(x_ref.at[rows(c)], xr.at[1, rows(c)], x2_s.at[c], x_r.at[1, c], to_f=fx2)
        for c in range(CHUNKS)
    ]
    x_to_8 = copy(x_ref, xr.at[3], x8_s, x8_r, to_f=fx8)
    fwd_0 = [
        copy(xr.at[0, rows(c)], xr.at[1, rows(c)], f0_s.at[c], x_r.at[1, c], to_f=fx3)
        for c in range(CHUNKS)
    ]
    fwd_1 = [
        copy(xr.at[1, rows(c)], xr.at[2, rows(c)], f1_s.at[c], x_r.at[2, c], to_f=fx6)
        for c in range(CHUNKS)
    ]

    def relay_0(c):
        @pl.when(odd)
        def _():
            arrived(xr.at[0, rows(c)], x_r.at[0, c])
            fwd_0[c].start()

    def relay_1(c):
        arrived(xr.at[1, rows(c)], x_r.at[1, c])
        fwd_1[c].start()

    def tiles(step):
        lax.fori_loop(0, N // TILE, lambda i, _: (step(i), 0)[1], 0)

    def tile(i):
        return pl.ds(pl.multiple_of(i * TILE, TILE), TILE)

    def split_g(i):
        gh[tile(i)], gl[tile(i)] = halves(g_ref[tile(i)])

    def split_w(i):
        for k in range(5):
            block = wg[pl.ds(i * 4, 4), k].reshape(TILE, N)
            wh[k, tile(i)], wl[k, tile(i)] = halves(block)

    def source(k):
        return x_ref if k == 0 else xr.at[k - 1]

    def to_outputs(k):
        def step(i):
            term = product(halves(source(k)[tile(i)]), (wh[k], wl[k]), 1, 0)
            out_ref[tile(i)] = term if k == 0 else out_ref[tile(i)] + term

        tiles(step)

    def to_products(k):
        def step(i):
            term = product((gh[tile(i)], gl[tile(i)]), (wh[k], wl[k]), 1, 1)
            if k == 0:
                dx_ref[tile(i)] = term
            else:
                pb[k - 1, tile(i)] = term

        tiles(step)

    def to_grad(k):
        def step(i):
            part = halves(source(k)[:, tile(i)])
            term = product(part, (gh[...], gl[...]), 0, 0)
            d[k, pl.ds(i * 2, 2)] = term.reshape(2, 2, 32, N)

        tiles(step)

    d_out = [copy(d.at[k, :, 1 - core], er.at[k], d_s.at[k], d_r.at[k], to_dp=sib) for k in range(6)]
    e_out = [
        [
            copy(e.at[k, :, at_x(q)], fr.at[k, q - 1], e_s.at[k, q - 1], e_r.at[k, q - 1], to_dp=dp_x(q))
            for q in (1, 3, 2)
        ]
        for k in range(6)
    ]
    h_out = [copy(fs.at[k, 1 - yh], hr.at[k], h_s.at[k], h_r.at[k], to_dp=far) for k in range(6)]
    scale = 1.0 / math.sqrt(N * 16)

    def sum_1(k):
        d_out[k].start()

    def sum_2(k):
        arrived(er.at[k], d_r.at[k])
        for y in range(2):
            for q in range(4):
                e[k, y, q] = d[k, y * 4 + q, core] + er[k, y * 4 + q]
        for c in e_out[k]:
            c.start()

    def sum_3(k):
        for q in range(3):
            arrived(fr.at[k, q], e_r.at[k, q])
        fs[k] = (e[k, :, x] + fr[k, 0]) + (fr[k, 1] + fr[k, 2])
        h_out[k].start()

    def sum_4(k):
        arrived(hr.at[k], h_r.at[k])
        total = (fs[k, yh] + hr[k]) * scale
        if k < 5:
            bg_ref[k] = total
        else:
            lr_out_ref[...] = total

    cy_out = copy(cp.at[1 - b3], cy, cy_s, cy_r, to_f=fx8)
    cs_out = [
        copy(cp.at[b3, zs(k)], cs.at[k - 1], cs_s.at[k - 1], cs_r.at[k - 1], to_f=b3 * 8 + zs(k))
        for k in range(1, 8)
    ]
    cg_out = [
        copy(cr, cf.at[b3, z], cg_s.at[k - 1], cg_r.at[z], to_f=b3 * 8 + zs(k)) for k in range(1, 8)
    ]
    ch_out = copy(cf.at[b3], cf.at[b3], ch_s, ch_r, to_f=fx8)

    def left_full():
        return lrg[:, 0:32].reshape(N, 256)

    def right_full(half):
        return lrg[:, 32 + 16 * half : 48 + 16 * half].reshape(256, 256)

    def codes_1():
        left = halves(left_full())
        right = [halves(right_full(h)) for h in range(2)]

        def step(i):
            codes = product(halves(x_ref[tile(i)]), left, 1, 0)
            grads = product((gh[tile(i), 0:256], gl[tile(i), 0:256]), right[0], 1, 1)
            grads += product((gh[tile(i), 256:512], gl[tile(i), 256:512]), right[1], 1, 1)
            cp[i // 2, pl.ds((i % 2) * 4, 4), :, 0:256] = codes.reshape(4, 32, 256)
            cp[i // 2, pl.ds((i % 2) * 4, 4), :, 256:512] = grads.reshape(4, 32, 256)

        tiles(step)
        cy_out.start()

    def codes_2():
        arrived(cy, cy_r)
        for q in range(8):
            cp[b3, q] = cp[b3, q] + cy[q]
        for c in cs_out:
            c.start()

    def codes_3():
        for k in range(7):
            arrived(cs.at[k], cs_r.at[k])
        total = cp[b3, z]
        for k in range(7):
            total += cs[k]
        cr[...] = total
        cf[b3, z] = total
        for c in cg_out:
            c.start()

    def codes_4():
        for k in range(1, 8):
            arrived(cf.at[b3, zs(k)], cg_r.at[zs(k)])
        ch_out.start()

    def codes_5():
        arrived(cf.at[1 - b3], ch_r)
        left = halves(left_full())
        right = [halves(right_full(h)) for h in range(2)]

        def codes_of(i):
            return cf[i // 2, pl.ds((i % 2) * 4, 4)].reshape(TILE, N)

        def step(i):
            both = codes_of(i)
            codes, grads = halves(both[:, 0:256]), halves(both[:, 256:512])
            for h in range(2):
                cols = slice(256 * h, 256 * (h + 1))
                out_ref[tile(i), cols] += product(codes, right[h], 1, 0)
            dx_ref[tile(i)] += product(grads, left, 1, 1)

        tiles(step)
        all_codes = cf[...].reshape(N, N)
        grads = halves(all_codes[:, 256:512])

        def left_step(i):
            term = product(halves(x_ref[:, tile(i)]), grads, 0, 0)
            d[5, pl.ds(i * 2, 2), :, :, 0:256] = term.reshape(2, 2, 32, 256)

        tiles(left_step)
        for h in range(2):
            part = halves(all_codes[:, 128 * h : 128 * (h + 1)])
            term = product(part, (gh[...], gl[...]), 0, 0).reshape(4, 2, 16, N)
            d[5, 4 * h : 4 * h + 4, :, 0:16, 256:512] = term[:, :, :, 0:256]
            d[5, 4 * h : 4 * h + 4, :, 16:32, 256:512] = term[:, :, :, 256:512]

    p4_out = [
        copy(pb.at[2, rows(c)], r4.at[rows(c)], p4_s.at[c], r4_r.at[c], to_f=fx6) for c in range(CHUNKS)
    ]
    p2_even = [
        copy(pb.at[1, rows(c)], rf2.at[rows(c)], p2_s.at[c], rf2_r.at[c], to_f=fx2)
        for c in range(CHUNKS)
    ]
    p2_odd = [
        copy(pb.at[1, rows(c)], r2.at[rows(c)], p2_s.at[c], r2_r.at[c], to_f=fx3) for c in range(CHUNKS)
    ]
    p1_out = [
        copy(pb.at[0, rows(c)], rf1.at[rows(c)], p1_s.at[c], rf1_r.at[c], to_f=fx1)
        for c in range(CHUNKS)
    ]
    p8_out = copy(pb.at[3], rf3, p8_s, rf3_r, to_f=fx8)

    def back_2(c):
        arrived(r4.at[rows(c)], r4_r.at[c])
        pb[1, rows(c)] = pb[1, rows(c)] + r4[rows(c)]
        pl.when(even)(p2_even[c].start)
        pl.when(odd)(p2_odd[c].start)

    def back_1(c):
        @pl.when(odd)
        def _():
            arrived(r2.at[rows(c)], r2_r.at[c])
            pb[0, rows(c)] = pb[0, rows(c)] + r2[rows(c)]
            p1_out[c].start()

    def back_0(c):
        arrived(rf1.at[rows(c)], rf1_r.at[c])
        dx_ref[rows(c)] += rf1[rows(c)]

        @pl.when(odd)
        def _():
            arrived(rf2.at[rows(c)], rf2_r.at[c])
            dx_ref[rows(c)] += rf2[rows(c)]

    lr_start()
    for c in range(CHUNKS):
        x_to_1[c].start()

        @pl.when(odd)
        def _():
            x_to_2[c].start()

    w_start()
    x_to_8.start()
    tiles(split_g)
    lr_relay()
    to_grad(0)
    sum_1(0)
    lr_third()
    lr_fourth()
    lr_finish()
    codes_1()
    relay_0(0)
    w_relay()
    relay_0(1)
    relay_0(2)
    codes_2()
    sum_2(0)
    relay_0(3)
    relay_1(0)
    w_third()
    relay_0(4)
    relay_1(1)
    relay_0(5)
    relay_1(2)
    relay_0(6)
    w_fourth()
    relay_1(3)
    relay_0(7)
    w_finish()
    tiles(split_w)
    to_products(3)
    for c in p4_out:
        c.start()
    relay_1(4)
    codes_3()
    to_products(2)
    to_products(1)

    @pl.when(even)
    def _():
        for c in p1_out:
            c.start()

    relay_1(5)
    to_products(4)
    p8_out.start()
    sum_3(0)
    to_products(0)
    to_outputs(0)
    relay_1(6)
    arrived(xr.at[3], x8_r)
    to_grad(4)
    sum_1(4)
    codes_4()
    relay_1(7)
    to_outputs(4)
    sum_2(4)

    @pl.when(even)
    def _():
        for c in range(CHUNKS):
            arrived(xr.at[0, rows(c)], x_r.at[0, c])

    back_2(0)
    to_grad(1)
    sum_1(1)
    back_2(1)
    codes_5()
    sum_1(5)
    back_2(2)
    to_grad(2)
    sum_1(2)
    back_1(0)
    sum_2(1)
    sum_2(5)
    sum_3(4)
    back_2(3)
    to_outputs(1)
    back_1(1)
    to_outputs(2)
    sum_2(2)
    back_2(4)
    for c in range(CHUNKS):
        arrived(xr.at[2, rows(c)], x_r.at[2, c])
    to_grad(3)
    sum_1(3)
    back_1(2)
    back_2(5)
    to_outputs(3)
    sum_2(3)
    for k in (1, 5, 2):
        sum_3(k)
    back_1(3)
    back_2(6)
    arrived(rf3, rf3_r)

    def add_8(i):
        dx_ref[tile(i)] += rf3[tile(i)]

    tiles(add_8)
    sum_3(3)
    back_1(4)
    back_2(7)
    for k in (0, 4, 1, 5, 2):
        sum_4(k)
    back_1(5)
    sum_4(3)
    back_0(0)
    back_1(6)
    back_0(1)
    back_1(7)
    for c in range(2, CHUNKS):
        back_0(c)

    lr_drain()
    w_drain()
    for c in x_to_1 + fwd_1 + p4_out + p1_out + cs_out + cg_out + d_out + h_out:
        c.wait_send()
    for group in e_out:
        for c in group:
            c.wait_send()
    for c in (x_to_8, cy_out, ch_out, p8_out):
        c.wait_send()

    @pl.when(odd)
    def _():
        for c in x_to_2 + fwd_0 + p2_odd:
            c.wait_send()

    @pl.when(even)
    def _():
        for c in p2_even:
            c.wait_send()


def on_device(inputs, partner_bits, block_weights, low_left, low_right, cotangent):
    my_bits = partner_bits[0]
    weights = block_weights[0]
    by_bit = [weights[:, 0]]
    for bit in range(4):
        chosen = weights[:, 1]
        for slot in range(1, 4):
            chosen = jnp.where(my_bits[slot] == bit, weights[:, 1 + slot], chosen)
        by_bit.append(chosen)
    by_bit = jnp.stack(by_bit)

    vmem = pl.BlockSpec(memory_space=pltpu.VMEM)
    hbm = pl.BlockSpec(memory_space=pl.ANY)
    dma = pltpu.SemaphoreType.DMA

    def buf(*shape, dtype=F32):
        return pltpu.VMEM(shape, dtype)

    outputs, input_grad, grads, low = pl.pallas_call(
        kernel,
        out_shape=(
            jax.ShapeDtypeStruct((N, N), F32),
            jax.ShapeDtypeStruct((N, N), F32),
            jax.ShapeDtypeStruct((5, 32, N), F32),
            jax.ShapeDtypeStruct((32, N), F32),
        ),
        in_specs=[vmem, vmem, hbm, hbm, hbm],
        out_specs=(vmem, vmem, vmem, vmem),
        scratch_shapes=[
            buf(16, 64, 256), buf(16, 5, 32, N),
            buf(5, N, N, dtype=BF16), buf(5, N, N, dtype=BF16),
            buf(N, N, dtype=BF16), buf(N, N, dtype=BF16), buf(4, N, N),
            buf(2, 8, 32, N), buf(8, 32, N), buf(7, 32, N), buf(32, N), buf(2, 8, 32, N),
            buf(4, N, N), buf(N, N), buf(N, N), buf(N, N), buf(N, N), buf(N, N),
            buf(6, 8, 2, 32, N), buf(6, 8, 32, N), buf(6, 2, 4, 32, N), buf(6, 3, 2, 32, N),
            buf(6, 2, 32, N), buf(6, 32, N),
            dma((4,)),
            dma((15,)), dma((16,)), dma((15,)), dma((16,)),
            dma((CHUNKS,)), dma((CHUNKS,)), dma, dma((CHUNKS,)), dma((CHUNKS,)), dma((3, CHUNKS)), dma,
            dma, dma, dma((7,)), dma((7,)), dma((7,)), dma((8,)), dma, dma,
            dma((CHUNKS,)), dma((CHUNKS,)), dma((CHUNKS,)), dma,
            dma((CHUNKS,)), dma((CHUNKS,)), dma((CHUNKS,)), dma((CHUNKS,)), dma,
            dma((6,)), dma((6,)), dma((6, 3)), dma((6, 3)), dma((6,)), dma((6,)),
        ],
        compiler_params=pltpu.CompilerParams(
            collective_id=0, has_side_effects=True, vmem_limit_bytes=60 << 20
        ),
    )(inputs, cotangent, by_bit, low_left[0], low_right[0])

    slots = [grads[0]]
    for slot in range(4):
        chosen = grads[1]
        for bit in range(1, 4):
            chosen = jnp.where(my_bits[slot] == bit, grads[1 + bit], chosen)
        slots.append(chosen)
    block_grads = jnp.stack(slots, axis=1)[None]
    left_grads = low[:, 0:256][None]
    right_grads = jnp.concatenate([low[0:16, 256:512], low[16:32, 256:512]], axis=1)[None]
    return outputs, input_grad, block_grads, left_grads, right_grads


def solution(mesh):
    in_specs = (
        P("dp", "feat"),
        P("feat", None),
        P("feat", "dp", None, None),
        P("feat", "dp", None),
        P("feat", "dp", None),
        P("dp", "feat"),
    )
    out_specs = (
        P("dp", "feat"),
        P("dp", "feat"),
        P("feat", "dp", None, None),
        P("feat", "dp", None),
        P("feat", "dp", None),
    )
    return jax.shard_map(on_device, mesh=mesh, in_specs=in_specs, out_specs=out_specs, check_vma=False)
```

time: 432 us -> 236 us (0.55)
  Pallas kernels: 0 us -> 212 us
  waiting for transfers between devices: 212 us -> 0 us
  starting transfers between devices: 76.7 us -> 0 us
  matrix products: 47.7 us -> 0 us
  local copies, waits for them, and re-layouts: 44.9 us -> 7.97 us
  other arithmetic: 20.1 us -> 2.66 us
  between operations: 19.4 us -> 10.5 us
  blocking collectives: 4.91 us -> 0 us
    pallas_call x0 -> x1, Pallas kernels: none -> 212 us  [on_device(): pl.pallas_call(kernel, out_shape=(jax.ShapeDtypeStruct((N, N), F32), jax....]
    ppermute x8 -> x0, waiting for transfers between devices: 114 us -> none  [swapped(): return lax.ppermute(block, axis, route)]
    all_to_all x7 -> x0, starting transfers between devices: 61.2 us -> none  [the longest x2 33 us: sent_to_all(): return lax.all_to_all(copies, axis, split_axis=0, concat_axis=0, tiled=True)]
    all_gather x2 -> x0, waiting for transfers between devices: 53.6 us -> none  [the longest x1 53.6 us: one_gather(): lines, at, finished = (lax.all_gather(vector, axis), 0, [])]
    dot_general x9 -> x0, matrix products: 47.7 us -> none  [the longest x1 12.4 us: on_device(): sparse = jnp.einsum('sri,iso->ro', sources, full_weights, precision=highest)]
    all_to_all x7 -> x0, waiting for transfers between devices: 43.4 us -> none  [the longest x3 20.2 us: summed_on_arrival(): lax.all_to_all(pieces, axis, split_axis=0, concat_axis=0, tiled=True)]
    ppermute x8 -> x0, starting transfers between devices: 15.4 us -> none  [swapped(): return lax.ppermute(block, axis, route)]
    reduce_sum x7 -> x0, other arithmetic: 11.7 us -> none  [the longest x4 8.96 us: summed_on_arrival(): return arrived.sum(axis=0)]
  transfers between devices with their start and end apart: 17 -> 0, of which waited for: 12 -> 0; matrix products, arithmetic and copies ran while one was open for 24% -> 0% of each run, Pallas kernels for 0% -> 0%
where the time goes in v1:
time: 236 us; the launch traced here: 233 us
  Pallas kernels  212 us (90%)
  between operations  10.5 us (4%)
  local copies, waits for them, and re-layouts  7.97 us (3%)
  other arithmetic  2.66 us (1%)
    pallas_call x1, Pallas kernels, on_device(): pl.pallas_call(kernel, out_shape=(jax.ShapeDtypeStruct((N, N), F32), jax....  212 us
    unnamed x18, local copies, waits for them, and re-layouts  5.96 us

profile of v1, /device:TPU:32, one launch (start us, length us, event | category | flops | bytes accessed | tf_op | source)
XLA Modules:
  0.0 233.1 jit_solution(5880487256147557956)
XLA Ops:
  0.6 0.0 copy-start
  0.6 0.9 fusion
  1.6 1.4 fusion.2
  4.9 1.0 bitcast_dynamic-update-slice_fusion.8
  7.8 0.0 copy-done
  11.8 0.0 copy-start.4
  11.8 0.7 copy-done.4
  12.5 212.0 %shard_map.101 = (f32[512,512]{1,0:T(8,128)}, f32[512,512]{1,0:T(8,128)}, f32[5,32,512]{2,1,0:T(8,128)}, f32[32,512]{1,0:T(8,128)}) custom-call(f32[512,512]{1,0:T(8,128)} %x_ref.1, f32[512,512]{1,0:T(8,128)} %g_ref.1, f32[5,32,512]{2,1,0:T(8,128)} %copy-done.4, f32[32,256]{1,0:T(8,128)} %bitcast.50, f32[16,512]{1,0:T(8,128)} %bitcast.51), custom_call_target="tpu_custom_call" | custom-call | tf_op jit(solution)/shard_map/pallas_call | solution.py:534
  224.5 0.0 copy-start.1
  224.5 0.0 copy-start.3
  224.5 0.9 bitcast_dynamic-update-slice_fusion.4
  227.4 1.0 bitcast_dynamic-update-slice_fusion.3
  228.4 0.0 copy-done.1
  228.5 0.0 copy-start.5
  228.5 0.0 copy-start.6
  228.5 0.8 copy-done.5
  229.3 0.6 slice_bitcast_fusion.1
  229.9 0.6 maximum_bitcast_fusion
  230.5 0.0 copy-done.3
  230.5 0.0 copy-start.2
  230.5 1.0 copy.21
  231.5 0.0 copy-done.6
  231.5 0.6 copy-done.2
  232.1 1.0 copy.22
  (7 shorter events, 0.1 us)
Async XLA Ops:
  0.6 7.2 %copy-start = (f32[1,32,5,512]{3,1,2,0:T(8,128)S(1)}, f32[1,32,5,512]{3,1,2,0:T(8,128)}, u32[]{:S(2)}) copy-start(f32[1,32,5,512]{3,1,2,0:T(8,128)} %param.8) | copy-start | bytes 983044
  11.8 0.7 copy-start.4
  224.5 3.9 %copy-start.1 = (f32[5,32,512]{2,1,0:T(8,128)S(1)}, f32[5,32,512]{2,1,0:T(8,128)}, u32[]{:S(2)}) copy-start(f32[5,32,512]{2,1,0:T(8,128)} %get-tuple-element.11) | copy-start | bytes 983044
  224.5 6.0 %copy-start.3 = (f32[512,512]{1,0:T(8,128)S(1)}, f32[512,512]{1,0:T(8,128)}, u32[]{:S(2)}) copy-start(f32[512,512]{1,0:T(8,128)} %get-tuple-element.24) | copy-start | bytes 3145732
  228.5 0.8 copy-start.5
  228.5 3.0 %copy-start.6 = (f32[32,5,512]{2,0,1:T(8,128)}, f32[32,5,512]{2,0,1:T(8,128)S(1)}, u32[]{:S(2)}) copy-start(f32[32,5,512]{2,0,1:T(8,128)S(1)} %bitcast_dynamic-update-slice_fusion) | copy-start | bytes 983044
  230.5 1.6 copy-start.2

commit v2 on v1

--- a/solution.py
+++ b/solution.py
@@ -30,12 +30,12 @@
 
 
 def kernel(
-    x_ref, g_ref, w_ref, l_ref, r_ref,
-    out_ref, dx_ref, bg_ref, lr_out_ref,
+    x_ref, g_ref, bits_ref, w_ref, l_ref, r_ref,
+    out_ref, dx_ref, bg_ref, left_ref, right_ref,
     lrg, wg, wh, wl, gh, gl, xr,
     cp, cy, cs, cr, cf,
     pb, r4, r2, rf1, rf2, rf3,
-    d, er, e, fr, fs, hr,
+    d, er, e, fr, fs, hr, sums,
     load_sem,
     lr_s, lr_r, w_s, w_r,
     x1_s, x2_s, x8_s, f0_s, f1_s, x_r, x8_r,
@@ -180,9 +180,17 @@
     def split_g(i):
         gh[tile(i)], gl[tile(i)] = halves(g_ref[tile(i)])
 
+    bits = [bits_ref[0, slot] for slot in range(4)]
+    slots = [0]
+    for bit in range(4):
+        slot = 1
+        for other in range(1, 4):
+            slot = jnp.where(bits[other] == bit, other + 1, slot)
+        slots.append(slot)
+
     def split_w(i):
         for k in range(5):
-            block = wg[pl.ds(i * 4, 4), k].reshape(TILE, N)
+            block = wg[pl.ds(i * 4, 4), slots[k]].reshape(TILE, N)
             wh[k, tile(i)], wl[k, tile(i)] = halves(block)
 
     def source(k):
@@ -244,10 +252,18 @@
     def sum_4(k):
         arrived(hr.at[k], h_r.at[k])
         total = (fs[k, yh] + hr[k]) * scale
-        if k < 5:
-            bg_ref[k] = total
+        if k == 0:
+            bg_ref[0] = total
+        elif k < 5:
+            sums[k - 1] = total
         else:
-            lr_out_ref[...] = total
+            left_ref[...] = total[:, 0:256]
+            right_ref[:, 0:256] = total[0:16, 256:512]
+            right_ref[:, 256:512] = total[16:32, 256:512]
+
+    def by_slot():
+        for slot in range(4):
+            bg_ref[1 + slot] = sums[bits[slot]]
 
     cy_out = copy(cp.at[1 - b3], cy, cy_s, cy_r, to_f=fx8)
     cs_out = [
@@ -371,125 +387,130 @@
             arrived(rf2.at[rows(c)], rf2_r.at[c])
             dx_ref[rows(c)] += rf2[rows(c)]
 
+    def start_x(c):
+        x_to_1[c].start()
+        pl.when(odd)(x_to_2[c].start)
+
     lr_start()
-    for c in range(CHUNKS):
-        x_to_1[c].start()
-
-        @pl.when(odd)
-        def _():
-            x_to_2[c].start()
-
+    for c in range(4):
+        start_x(c)
     w_start()
-    x_to_8.start()
     tiles(split_g)
     lr_relay()
+    lr_third()
+    relay_0(0)
+    lr_fourth()
+    lr_finish()
+    w_relay()
+    codes_1()
+    x_to_8.start()
+    relay_0(1)
     to_grad(0)
     sum_1(0)
-    lr_third()
-    lr_fourth()
-    lr_finish()
-    codes_1()
-    relay_0(0)
-    w_relay()
-    relay_0(1)
     relay_0(2)
+    relay_1(0)
+    relay_0(3)
+    relay_1(1)
+    w_third()
     codes_2()
+    for c in range(4, CHUNKS):
+        start_x(c)
+    relay_1(2)
+    relay_1(3)
+    relay_0(4)
     sum_2(0)
-    relay_0(3)
-    relay_1(0)
-    w_third()
-    relay_0(4)
-    relay_1(1)
     relay_0(5)
-    relay_1(2)
+    codes_3()
     relay_0(6)
+    relay_1(4)
     w_fourth()
-    relay_1(3)
     relay_0(7)
     w_finish()
     tiles(split_w)
     to_products(3)
     for c in p4_out:
         c.start()
-    relay_1(4)
-    codes_3()
+    relay_1(5)
     to_products(2)
     to_products(1)
-
-    @pl.when(even)
-    def _():
-        for c in p1_out:
-            c.start()
-
-    relay_1(5)
+    relay_1(6)
+
+    def back_20(c):
+        back_2(c)
+        pl.when(even)(p1_out[c].start)
+
+    back_20(0)
+    relay_1(7)
+    back_20(1)
+    sum_3(0)
     to_products(4)
     p8_out.start()
-    sum_3(0)
-    to_products(0)
-    to_outputs(0)
-    relay_1(6)
+    back_20(2)
     arrived(xr.at[3], x8_r)
     to_grad(4)
     sum_1(4)
-    codes_4()
-    relay_1(7)
-    to_outputs(4)
-    sum_2(4)
+    back_1(0)
+    back_20(3)
 
     @pl.when(even)
     def _():
         for c in range(CHUNKS):
             arrived(xr.at[0, rows(c)], x_r.at[0, c])
 
-    back_2(0)
     to_grad(1)
     sum_1(1)
-    back_2(1)
-    codes_5()
-    sum_1(5)
-    back_2(2)
+    codes_4()
+    back_1(1)
+    back_20(4)
     to_grad(2)
     sum_1(2)
-    back_1(0)
+    sum_2(4)
+    back_1(2)
+    to_products(0)
+    to_outputs(0)
+    back_20(5)
+    to_outputs(4)
     sum_2(1)
-    sum_2(5)
-    sum_3(4)
-    back_2(3)
-    to_outputs(1)
-    back_1(1)
-    to_outputs(2)
-    sum_2(2)
-    back_2(4)
+    back_1(3)
     for c in range(CHUNKS):
         arrived(xr.at[2, rows(c)], x_r.at[2, c])
     to_grad(3)
     sum_1(3)
-    back_1(2)
-    back_2(5)
+    back_20(6)
+    codes_5()
+    sum_1(5)
+    sum_2(2)
+    sum_3(4)
+    back_1(4)
+    back_20(7)
+    to_outputs(1)
+    sum_2(3)
+    back_1(5)
+    sum_2(5)
+    to_outputs(2)
+    sum_3(1)
+    sum_3(2)
+    back_1(6)
+    back_0(0)
     to_outputs(3)
-    sum_2(3)
-    for k in (1, 5, 2):
-        sum_3(k)
-    back_1(3)
-    back_2(6)
     arrived(rf3, rf3_r)
 
     def add_8(i):
         dx_ref[tile(i)] += rf3[tile(i)]
 
     tiles(add_8)
+    back_1(7)
+    back_0(1)
     sum_3(3)
-    back_1(4)
-    back_2(7)
-    for k in (0, 4, 1, 5, 2):
+    sum_3(5)
+    back_0(2)
+    for k in (0, 4, 1, 2):
         sum_4(k)
-    back_1(5)
+    back_0(3)
     sum_4(3)
-    back_0(0)
-    back_1(6)
-    back_0(1)
-    back_1(7)
-    for c in range(2, CHUNKS):
+    by_slot()
+    sum_4(5)
+    for c in range(4, CHUNKS):
         back_0(c)
 
     lr_drain()
@@ -514,33 +535,26 @@
 
 
 def on_device(inputs, partner_bits, block_weights, low_left, low_right, cotangent):
-    my_bits = partner_bits[0]
-    weights = block_weights[0]
-    by_bit = [weights[:, 0]]
-    for bit in range(4):
-        chosen = weights[:, 1]
-        for slot in range(1, 4):
-            chosen = jnp.where(my_bits[slot] == bit, weights[:, 1 + slot], chosen)
-        by_bit.append(chosen)
-    by_bit = jnp.stack(by_bit)
-
+    slots = jnp.swapaxes(block_weights[0], 0, 1)
     vmem = pl.BlockSpec(memory_space=pltpu.VMEM)
+    smem = pl.BlockSpec(memory_space=pltpu.SMEM)
     hbm = pl.BlockSpec(memory_space=pl.ANY)
     dma = pltpu.SemaphoreType.DMA
 
     def buf(*shape, dtype=F32):
         return pltpu.VMEM(shape, dtype)
 
-    outputs, input_grad, grads, low = pl.pallas_call(
+    outputs, input_grad, grads, left_grads, right_grads = pl.pallas_call(
         kernel,
         out_shape=(
             jax.ShapeDtypeStruct((N, N), F32),
             jax.ShapeDtypeStruct((N, N), F32),
             jax.ShapeDtypeStruct((5, 32, N), F32),
-            jax.ShapeDtypeStruct((32, N), F32),
+            jax.ShapeDtypeStruct((32, 256), F32),
+            jax.ShapeDtypeStruct((16, N), F32),
         ),
-        in_specs=[vmem, vmem, hbm, hbm, hbm],
-        out_specs=(vmem, vmem, vmem, vmem),
+        in_specs=[vmem, vmem, smem, hbm, hbm, hbm],
+        out_specs=(vmem, vmem, vmem, vmem, vmem),
         scratch_shapes=[
             buf(16, 64, 256), buf(16, 5, 32, N),
             buf(5, N, N, dtype=BF16), buf(5, N, N, dtype=BF16),
@@ -548,7 +562,7 @@
             buf(2, 8, 32, N), buf(8, 32, N), buf(7, 32, N), buf(32, N), buf(2, 8, 32, N),
             buf(4, N, N), buf(N, N), buf(N, N), buf(N, N), buf(N, N), buf(N, N),
             buf(6, 8, 2, 32, N), buf(6, 8, 32, N), buf(6, 2, 4, 32, N), buf(6, 3, 2, 32, N),
-            buf(6, 2, 32, N), buf(6, 32, N),
+            buf(6, 2, 32, N), buf(6, 32, N), buf(4, 32, N),
             dma((4,)),
             dma((15,)), dma((16,)), dma((15,)), dma((16,)),
             dma((CHUNKS,)), dma((CHUNKS,)), dma, dma((CHUNKS,)), dma((CHUNKS,)), dma((3, CHUNKS)), dma,
@@ -560,18 +574,10 @@
         compiler_params=pltpu.CompilerParams(
             collective_id=0, has_side_effects=True, vmem_limit_bytes=60 << 20
         ),
-    )(inputs, cotangent, by_bit, low_left[0], low_right[0])
-
-    slots = [grads[0]]
-    for slot in range(4):
-        chosen = grads[1]
-        for bit in range(1, 4):
-            chosen = jnp.where(my_bits[slot] == bit, grads[1 + bit], chosen)
-        slots.append(chosen)
-    block_grads = jnp.stack(slots, axis=1)[None]
-    left_grads = low[:, 0:256][None]
-    right_grads = jnp.concatenate([low[0:16, 256:512], low[16:32, 256:512]], axis=1)[None]
-    return outputs, input_grad, block_grads, left_grads, right_grads
+    )(inputs, cotangent, partner_bits, slots, low_left[0], low_right[0])
+
+    block_grads = jnp.swapaxes(grads, 0, 1)[None]
+    return outputs, input_grad, block_grads, left_grads[None], right_grads[None]
 
 
 def solution(mesh):

time: 236 us -> 196 us (0.83)
  Pallas kernels: 212 us -> 186 us
  between operations: 10.5 us -> 0.65 us
  other arithmetic: 2.66 us -> 0 us
    pallas_call x1, Pallas kernels: 212 us -> 186 us  [on_device(): pl.pallas_call(kernel, out_shape=(jax.ShapeDtypeStruct((N, N), F32), jax....]
    unnamed x18 -> x13, local copies, waits for them, and re-layouts: 5.96 us -> 5.66 us
where the time goes in v2:
time: 196 us; the launch traced here: 192 us
  Pallas kernels  186 us (95%)
  local copies, waits for them, and re-layouts  5.66 us (3%)
    pallas_call x1, Pallas kernels, on_device(): pl.pallas_call(kernel, out_shape=(jax.ShapeDtypeStruct((N, N), F32), jax....  186 us
    unnamed x13, local copies, waits for them, and re-layouts  5.66 us

profile of v2, /device:TPU:32, one launch (start us, length us, event | category | flops | bytes accessed | tf_op | source)
XLA Modules:
  0.0 192.1 jit_solution(769238627019038675)
XLA Ops:
  0.6 185.8 %shard_map.101 = (f32[512,512]{1,0:T(8,128)}, f32[512,512]{1,0:T(8,128)}, f32[5,32,512]{2,1,0:T(8,128)}, f32[32,256]{1,0:T(8,128)}, f32[16,512]{1,0:T(8,128)}) custom-call(f32[512,512]{1,0:T(8,128)} %x_ref.1, f32[512,512]{1,0:T(8,128)} %g_ref.1, s32[1,4]{1,0:T(1,128)} %bits_ref.1, f32[5,32,512]{2,1,0:T(8,128)} %bitcast.11, f32[32,256]{1,0:T(8,128)} %bitcast.12, ...), custom_call_target="tpu_custom_call" | custom-call | tf_op jit(solution)/shard_map/pallas_call | solution.py:547
  186.5 0.0 copy-start
  186.5 2.4 %copy.16 = f32[512,512]{1,0:T(8,128)} copy(f32[512,512]{1,0:T(8,128)} %get-tuple-element.20) | data formatting | bytes 2097152
  188.8 0.0 copy-done
  188.8 0.0 copy-start.1
  188.8 1.0 copy.17
  189.8 0.2 copy-done.1
  190.0 0.0 copy-start.3
  190.0 0.7 copy.18
  190.7 0.0 copy-done.3
  190.8 0.0 copy-start.2
  190.8 0.6 copy.19
  191.4 0.2 copy-done.2
  191.5 0.6 copy.20
Async XLA Ops:
  186.5 2.4 %copy-start = (f32[512,512]{1,0:T(8,128)S(1)}, f32[512,512]{1,0:T(8,128)}, u32[]{:S(2)}) copy-start(f32[512,512]{1,0:T(8,128)} %get-tuple-element.21) | copy-start | bytes 3145732
  188.8 1.2 copy-start.1
  190.0 0.8 copy-start.3
  190.8 0.8 copy-start.2

commit v3 on v2

--- a/solution.py
+++ b/solution.py
@@ -33,13 +33,13 @@
     x_ref, g_ref, bits_ref, w_ref, l_ref, r_ref,
     out_ref, dx_ref, bg_ref, left_ref, right_ref,
     lrg, wg, wh, wl, gh, gl, xr,
-    cp, cy, cs, cr, cf,
+    cp, cy, au, ad, cf,
     pb, r4, r2, rf1, rf2, rf3,
     d, er, e, fr, fs, hr, sums,
     load_sem,
     lr_s, lr_r, w_s, w_r,
     x1_s, x2_s, x8_s, f0_s, f1_s, x_r, x8_r,
-    cy_s, cy_r, cs_s, cs_r, cg_s, cg_r, ch_s, ch_r,
+    cy_s, cy_r, au_s, au_r, ad_s, ad_r, gu_s, gu_r, gd_s, gd_r, ch_s, ch_r,
     p4_s, p2_s, p1_s, p8_s, r4_r, r2_r, rf1_r, rf2_r, rf3_r,
     d_s, d_r, e_s, e_r, h_s, h_r,
 ):
@@ -125,11 +125,10 @@
                 arrived(whole.at[slot], recv.at[slot])
                 c.start()
 
-        def finish():
-            for y in range(2):
-                for k in range(4):
-                    slot = y * 8 + k * 2 + 1 - core
-                    arrived(whole.at[slot], recv.at[slot])
+        def finish(y):
+            for k in range(4):
+                slot = y * 8 + k * 2 + 1 - core
+                arrived(whole.at[slot], recv.at[slot])
 
         def drain():
             for c in first + second + [c for _, c in third + fourth]:
@@ -181,17 +180,21 @@
         gh[tile(i)], gl[tile(i)] = halves(g_ref[tile(i)])
 
     bits = [bits_ref[0, slot] for slot in range(4)]
-    slots = [0]
-    for bit in range(4):
-        slot = 1
-        for other in range(1, 4):
-            slot = jnp.where(bits[other] == bit, other + 1, slot)
-        slots.append(slot)
-
-    def split_w(i):
-        for k in range(5):
-            block = wg[pl.ds(i * 4, 4), slots[k]].reshape(TILE, N)
-            wh[k, tile(i)], wl[k, tile(i)] = halves(block)
+
+    def split_w(half):
+        def step(i):
+            t = 2 * half + i
+            by_slot = [halves(wg[pl.ds(t * 4, 4), slot].reshape(TILE, N)) for slot in range(5)]
+            wh[0, tile(t)], wl[0, tile(t)] = by_slot[0]
+            for bit in range(4):
+                high, low = by_slot[1]
+                for other in range(1, 4):
+                    here = bits[other] == bit
+                    high = jnp.where(here, by_slot[1 + other][0], high)
+                    low = jnp.where(here, by_slot[1 + other][1], low)
+                wh[1 + bit, tile(t)], wl[1 + bit, tile(t)] = high, low
+
+        lax.fori_loop(0, 2, lambda i, _: (step(i), 0)[1], 0)
 
     def source(k):
         return x_ref if k == 0 else xr.at[k - 1]
@@ -203,13 +206,15 @@
 
         tiles(step)
 
-    def to_products(k):
+    def to_products(k, half):
         def step(i):
-            term = product((gh[tile(i)], gl[tile(i)]), (wh[k], wl[k]), 1, 1)
+            mine = pl.ds(pl.multiple_of(half * 256, 256), 256)
+            term = product((gh[tile(i)], gl[tile(i)]), (wh[k, mine], wl[k, mine]), 1, 1)
             if k == 0:
-                dx_ref[tile(i)] = term
+                dx_ref[tile(i), mine] = term
             else:
-                pb[k - 1, tile(i)] = term
+                pb[k - 1, 2 * half, tile(i)] = term[:, 0:128]
+                pb[k - 1, 2 * half + 1, tile(i)] = term[:, 128:256]
 
         tiles(step)
 
@@ -266,14 +271,35 @@
             bg_ref[1 + slot] = sums[bits[slot]]
 
     cy_out = copy(cp.at[1 - b3], cy, cy_s, cy_r, to_f=fx8)
+    up, down = b3 * 8 + zs(1), b3 * 8 + zs(7)
+    part = [pl.ds(0, 16), pl.ds(16, 16)]
+
+    def both_ways(pick, land, sems, t):
+        if t == 0 and land is not None:
+            return [
+                copy(pick(4).at[part[0]], land[0].at[0, part[0]], sems[0].at[0], sems[1].at[0], to_f=up),
+                copy(pick(4).at[part[1]], land[1].at[0, part[1]], sems[2].at[0], sems[3].at[0], to_f=down),
+            ]
+        if land is not None:
+            return [
+                copy(pick(4 - t), land[0].at[t], sems[0].at[t], sems[1].at[t], to_f=up),
+                copy(pick(4 + t), land[1].at[t], sems[2].at[t], sems[3].at[t], to_f=down),
+            ]
+        one, two = pick(8 - t), pick(t)
+        if t == 3:
+            one, two = one.at[part[0]], two.at[part[1]]
+        return [
+            copy(one, one, sems[0].at[t], sems[1].at[t], to_f=up),
+            copy(two, two, sems[2].at[t], sems[3].at[t], to_f=down),
+        ]
+
     cs_out = [
-        copy(cp.at[b3, zs(k)], cs.at[k - 1], cs_s.at[k - 1], cs_r.at[k - 1], to_f=b3 * 8 + zs(k))
-        for k in range(1, 8)
-    ]
-    cg_out = [
-        copy(cr, cf.at[b3, z], cg_s.at[k - 1], cg_r.at[z], to_f=b3 * 8 + zs(k)) for k in range(1, 8)
-    ]
-    ch_out = copy(cf.at[b3], cf.at[b3], ch_s, ch_r, to_f=fx8)
+        both_ways(lambda k: cp.at[b3, zs(k)], (au, ad), (au_s, au_r, ad_s, ad_r), t) for t in range(4)
+    ]
+    cg_out = [both_ways(lambda k: cf.at[b3, zs(k)], None, (gu_s, gu_r, gd_s, gd_r), t) for t in range(4)]
+    ch_out = [
+        copy(cf.at[b3, zs(k)], cf.at[b3, zs(k)], ch_s.at[k], ch_r.at[zs(k)], to_f=fx8) for k in range(8)
+    ]
 
     def left_full():
         return lrg[:, 0:32].reshape(N, 256)
@@ -299,27 +325,44 @@
         arrived(cy, cy_r)
         for q in range(8):
             cp[b3, q] = cp[b3, q] + cy[q]
-        for c in cs_out:
+        for c in cs_out[0]:
             c.start()
 
+    def codes_sum(t):
+        if t == 1:
+            arrived(au.at[0, part[0]], au_r.at[0])
+            arrived(ad.at[0, part[1]], ad_r.at[0])
+            cp[b3, zs(3), 0:16] = cp[b3, zs(3), 0:16] + au[0, 0:16]
+            cp[b3, zs(5), 16:32] = cp[b3, zs(5), 16:32] + ad[0, 16:32]
+        else:
+            arrived(au.at[t - 1], au_r.at[t - 1])
+            arrived(ad.at[t - 1], ad_r.at[t - 1])
+            cp[b3, zs(4 - t)] = cp[b3, zs(4 - t)] + au[t - 1]
+            cp[b3, zs(4 + t)] = cp[b3, zs(4 + t)] + ad[t - 1]
+        for c in cs_out[t]:
+            c.start()
+
     def codes_3():
-        for k in range(7):
-            arrived(cs.at[k], cs_r.at[k])
-        total = cp[b3, z]
-        for k in range(7):
-            total += cs[k]
-        cr[...] = total
-        cf[b3, z] = total
-        for c in cg_out:
+        arrived(au.at[3], au_r.at[3])
+        arrived(ad.at[3], ad_r.at[3])
+        cf[b3, z] = (cp[b3, z] + au[3]) + ad[3]
+        for c in cg_out[0] + [ch_out[0]]:
             c.start()
 
+    def codes_pass(t):
+        arrived(cf.at[b3, zs(8 - t)], gu_r.at[t - 1])
+        arrived(cf.at[b3, zs(t)], gd_r.at[t - 1])
+        for c in cg_out[t] + [ch_out[8 - t], ch_out[t]]:
+            c.start()
+
     def codes_4():
-        for k in range(1, 8):
-            arrived(cf.at[b3, zs(k)], cg_r.at[zs(k)])
-        ch_out.start()
+        arrived(cf.at[b3, zs(4), part[0]], gu_r.at[3])
+        arrived(cf.at[b3, zs(4), part[1]], gd_r.at[3])
+        ch_out[4].start()
 
     def codes_5():
-        arrived(cf.at[1 - b3], ch_r)
+        for k in range(8):
+            arrived(cf.at[1 - b3, k], ch_r.at[k])
         left = halves(left_full())
         right = [halves(right_full(h)) for h in range(2)]
 
@@ -344,183 +387,238 @@
 
         tiles(left_step)
         for h in range(2):
-            part = halves(all_codes[:, 128 * h : 128 * (h + 1)])
-            term = product(part, (gh[...], gl[...]), 0, 0).reshape(4, 2, 16, N)
+            some = halves(all_codes[:, 128 * h : 128 * (h + 1)])
+            term = product(some, (gh[...], gl[...]), 0, 0).reshape(4, 2, 16, N)
             d[5, 4 * h : 4 * h + 4, :, 0:16, 256:512] = term[:, :, :, 0:256]
             d[5, 4 * h : 4 * h + 4, :, 16:32, 256:512] = term[:, :, :, 256:512]
 
-    p4_out = [
-        copy(pb.at[2, rows(c)], r4.at[rows(c)], p4_s.at[c], r4_r.at[c], to_f=fx6) for c in range(CHUNKS)
-    ]
-    p2_even = [
-        copy(pb.at[1, rows(c)], rf2.at[rows(c)], p2_s.at[c], rf2_r.at[c], to_f=fx2)
-        for c in range(CHUNKS)
-    ]
-    p2_odd = [
-        copy(pb.at[1, rows(c)], r2.at[rows(c)], p2_s.at[c], r2_r.at[c], to_f=fx3) for c in range(CHUNKS)
-    ]
-    p1_out = [
-        copy(pb.at[0, rows(c)], rf1.at[rows(c)], p1_s.at[c], rf1_r.at[c], to_f=fx1)
-        for c in range(CHUNKS)
-    ]
+    def block(c):
+        return (c // 2 + 2 * yh) % 4
+
+    def chunk(ref, c):
+        return ref.at[block(c), pl.ds((c % 2) * 256, 256)]
+
+    def back(bit, ref, send, recv, to):
+        return [
+            copy(chunk(pb.at[bit], c), chunk(ref, c), send.at[c], recv.at[c], to_f=to)
+            for c in range(CHUNKS)
+        ]
+
+    p4_out = back(2, r4, p4_s, r4_r, fx6)
+    p2_even = back(1, rf2, p2_s, rf2_r, fx2)
+    p2_odd = back(1, r2, p2_s, r2_r, fx3)
+    p1_out = back(0, rf1, p1_s, rf1_r, fx1)
     p8_out = copy(pb.at[3], rf3, p8_s, rf3_r, to_f=fx8)
 
+    def add_to(bit, ref, c):
+        part = (block(c), pl.ds((c % 2) * 256, 256))
+        pb[(bit, *part)] = pb[(bit, *part)] + ref[part]
+
+    def add_to_dx(ref, c):
+        here = (pl.ds((c % 2) * 256, 256), pl.ds(pl.multiple_of(block(c) * 128, 128), 128))
+        dx_ref[here] = dx_ref[here] + ref[block(c), pl.ds((c % 2) * 256, 256)]
+
     def back_2(c):
-        arrived(r4.at[rows(c)], r4_r.at[c])
-        pb[1, rows(c)] = pb[1, rows(c)] + r4[rows(c)]
+        arrived(chunk(r4, c), r4_r.at[c])
+        add_to(1, r4, c)
         pl.when(even)(p2_even[c].start)
         pl.when(odd)(p2_odd[c].start)
 
     def back_1(c):
         @pl.when(odd)
         def _():
-            arrived(r2.at[rows(c)], r2_r.at[c])
-            pb[0, rows(c)] = pb[0, rows(c)] + r2[rows(c)]
+            arrived(chunk(r2, c), r2_r.at[c])
+            add_to(0, r2, c)
             p1_out[c].start()
 
     def back_0(c):
-        arrived(rf1.at[rows(c)], rf1_r.at[c])
-        dx_ref[rows(c)] += rf1[rows(c)]
+        arrived(chunk(rf1, c), rf1_r.at[c])
+        add_to_dx(rf1, c)
 
         @pl.when(odd)
         def _():
-            arrived(rf2.at[rows(c)], rf2_r.at[c])
-            dx_ref[rows(c)] += rf2[rows(c)]
+            arrived(chunk(rf2, c), rf2_r.at[c])
+            add_to_dx(rf2, c)
 
     def start_x(c):
         x_to_1[c].start()
         pl.when(odd)(x_to_2[c].start)
 
+    def start_p(c):
+        p4_out[c].start()
+
+    def add_8():
+        arrived(rf3, rf3_r)
+        for q in range(4):
+            dx_ref[:, 128 * q : 128 * (q + 1)] = dx_ref[:, 128 * q : 128 * (q + 1)] + rf3[q]
+
+    def x0_here():
+        @pl.when(even)
+        def _():
+            for c in range(CHUNKS):
+                arrived(xr.at[0, rows(c)], x_r.at[0, c])
+
+    def x2_here():
+        for c in range(CHUNKS):
+            arrived(xr.at[2, rows(c)], x_r.at[2, c])
+
+    def low_1():
+        lr_third()
+        lr_fourth()
+        lr_finish(0)
+        lr_finish(1)
+        codes_1()
+        x_to_8.start()
+
+    def weights(half):
+        w_finish(half)
+        split_w(half)
+
+    def x8_grad():
+        arrived(xr.at[3], x8_r)
+        to_grad(4)
+        sum_1(4)
+
     lr_start()
-    for c in range(4):
-        start_x(c)
-    w_start()
+    start_x(0)
+    start_x(1)
     tiles(split_g)
     lr_relay()
-    lr_third()
-    relay_0(0)
-    lr_fourth()
-    lr_finish()
-    w_relay()
-    codes_1()
-    x_to_8.start()
-    relay_0(1)
+    w_start()
+    low_1()
     to_grad(0)
     sum_1(0)
+    relay_0(0)
+    start_x(2)
+    relay_0(1)
+    start_x(3)
+    relay_1(0)
+    w_relay()
+    codes_2()
     relay_0(2)
-    relay_1(0)
-    relay_0(3)
+    start_x(4)
     relay_1(1)
     w_third()
-    codes_2()
-    for c in range(4, CHUNKS):
-        start_x(c)
+    weights(yh)
+    to_products(3, yh)
+    start_p(0); start_p(1)
+    to_products(2, yh)
+    to_products(1, yh)
+    codes_sum(1)
+    relay_0(3)
+    start_x(5)
     relay_1(2)
+    back_2(0)
+    start_p(2)
+    pl.when(even)(p1_out[0].start)
+    sum_2(0)
+    codes_sum(2)
+    relay_0(4)
+    start_x(6)
     relay_1(3)
-    relay_0(4)
-    sum_2(0)
+    back_2(1)
+    start_p(3)
+    pl.when(even)(p1_out[1].start)
+    back_1(0)
+    w_fourth()
+    weights(1 - yh)
+    to_products(3, 1 - yh)
+    to_products(2, 1 - yh)
+    to_products(1, 1 - yh)
+    codes_sum(3)
     relay_0(5)
+    start_x(7)
+    relay_1(4)
+    back_2(2)
+    start_p(4)
+    pl.when(even)(p1_out[2].start)
+    back_1(1)
+    x8_grad()
+    to_products(4, 0)
+    to_products(4, 1)
+    p8_out.start()
     codes_3()
     relay_0(6)
-    relay_1(4)
-    w_fourth()
+    relay_1(5)
+    back_2(3)
+    start_p(5)
+    pl.when(even)(p1_out[3].start)
+    back_1(2)
+    to_products(0, 0)
+    to_products(0, 1)
+    sum_2(4)
+    codes_pass(1)
     relay_0(7)
-    w_finish()
-    tiles(split_w)
-    to_products(3)
-    for c in p4_out:
-        c.start()
-    relay_1(5)
-    to_products(2)
-    to_products(1)
     relay_1(6)
-
-    def back_20(c):
-        back_2(c)
-        pl.when(even)(p1_out[c].start)
-
-    back_20(0)
-    relay_1(7)
-    back_20(1)
-    sum_3(0)
-    to_products(4)
-    p8_out.start()
-    back_20(2)
-    arrived(xr.at[3], x8_r)
-    to_grad(4)
-    sum_1(4)
-    back_1(0)
-    back_20(3)
-
-    @pl.when(even)
-    def _():
-        for c in range(CHUNKS):
-            arrived(xr.at[0, rows(c)], x_r.at[0, c])
-
+    back_2(4)
+    start_p(6)
+    pl.when(even)(p1_out[4].start)
+    back_1(3)
+    back_0(0)
+    x0_here()
     to_grad(1)
     sum_1(1)
-    codes_4()
-    back_1(1)
-    back_20(4)
+    codes_pass(2)
+    relay_1(7)
+    back_2(5)
+    start_p(7)
+    pl.when(even)(p1_out[5].start)
+    back_1(4)
+    back_0(1)
     to_grad(2)
     sum_1(2)
-    sum_2(4)
-    back_1(2)
-    to_products(0)
+    sum_3(0)
+    codes_pass(3)
+    back_2(6)
+    pl.when(even)(p1_out[6].start)
+    back_1(5)
+    back_0(2)
+    sum_2(1)
     to_outputs(0)
-    back_20(5)
-    to_outputs(4)
-    sum_2(1)
-    back_1(3)
-    for c in range(CHUNKS):
-        arrived(xr.at[2, rows(c)], x_r.at[2, c])
+    codes_4()
+    back_2(7)
+    pl.when(even)(p1_out[7].start)
+    back_1(6)
+    back_0(3)
+    sum_2(2)
+    sum_3(4)
+    to_outputs(1)
+    back_1(7)
+    back_0(4)
+    x2_here()
     to_grad(3)
     sum_1(3)
-    back_20(6)
     codes_5()
     sum_1(5)
-    sum_2(2)
-    sum_3(4)
-    back_1(4)
-    back_20(7)
-    to_outputs(1)
+    sum_3(1)
+    back_0(5)
     sum_2(3)
-    back_1(5)
+    sum_3(2)
+    to_outputs(4)
     sum_2(5)
+    back_0(6)
+    sum_3(3)
     to_outputs(2)
-    sum_3(1)
-    sum_3(2)
-    back_1(6)
-    back_0(0)
+    add_8()
+    sum_3(5)
+    back_0(7)
     to_outputs(3)
-    arrived(rf3, rf3_r)
-
-    def add_8(i):
-        dx_ref[tile(i)] += rf3[tile(i)]
-
-    tiles(add_8)
-    back_1(7)
-    back_0(1)
-    sum_3(3)
-    sum_3(5)
-    back_0(2)
-    for k in (0, 4, 1, 2):
-        sum_4(k)
-    back_0(3)
+    sum_4(0)
+    sum_4(1)
+    sum_4(2)
     sum_4(3)
+    sum_4(4)
+    sum_4(5)
     by_slot()
-    sum_4(5)
-    for c in range(4, CHUNKS):
-        back_0(c)
 
     lr_drain()
     w_drain()
-    for c in x_to_1 + fwd_1 + p4_out + p1_out + cs_out + cg_out + d_out + h_out:
+    for c in x_to_1 + fwd_1 + p4_out + p1_out + d_out + h_out:
         c.wait_send()
-    for group in e_out:
+    for group in e_out + cs_out + cg_out + [ch_out]:
         for c in group:
             c.wait_send()
-    for c in (x_to_8, cy_out, ch_out, p8_out):
+    for c in (x_to_8, cy_out, p8_out):
         c.wait_send()
 
     @pl.when(odd)
@@ -559,14 +657,14 @@
             buf(16, 64, 256), buf(16, 5, 32, N),
             buf(5, N, N, dtype=BF16), buf(5, N, N, dtype=BF16),
             buf(N, N, dtype=BF16), buf(N, N, dtype=BF16), buf(4, N, N),
-            buf(2, 8, 32, N), buf(8, 32, N), buf(7, 32, N), buf(32, N), buf(2, 8, 32, N),
-            buf(4, N, N), buf(N, N), buf(N, N), buf(N, N), buf(N, N), buf(N, N),
+            buf(2, 8, 32, N), buf(8, 32, N), buf(4, 32, N), buf(4, 32, N), buf(2, 8, 32, N),
+            buf(4, 4, N, 128), *[buf(4, N, 128)] * 5,
             buf(6, 8, 2, 32, N), buf(6, 8, 32, N), buf(6, 2, 4, 32, N), buf(6, 3, 2, 32, N),
             buf(6, 2, 32, N), buf(6, 32, N), buf(4, 32, N),
             dma((4,)),
             dma((15,)), dma((16,)), dma((15,)), dma((16,)),
             dma((CHUNKS,)), dma((CHUNKS,)), dma, dma((CHUNKS,)), dma((CHUNKS,)), dma((3, CHUNKS)), dma,
-            dma, dma, dma((7,)), dma((7,)), dma((7,)), dma((8,)), dma, dma,
+            dma, dma, *[dma((4,))] * 8, dma((8,)), dma((8,)),
             dma((CHUNKS,)), dma((CHUNKS,)), dma((CHUNKS,)), dma,
             dma((CHUNKS,)), dma((CHUNKS,)), dma((CHUNKS,)), dma((CHUNKS,)), dma,
             dma((6,)), dma((6,)), dma((6, 3)), dma((6, 3)), dma((6,)), dma((6,)),

time: 196 us -> 180 us (0.918); the launches traced: 192 us -> 180 us
  Pallas kernels: 186 us -> 173 us
    pallas_call x1, Pallas kernels: 186 us -> 173 us  [on_device(): pl.pallas_call(kernel, out_shape=(jax.ShapeDtypeStruct((N, N), F32), jax....]
where the time goes in v3:
time: 180 us
  Pallas kernels  173 us (96%)
  local copies, waits for them, and re-layouts  5.66 us (3%)
    pallas_call x1, Pallas kernels, on_device(): pl.pallas_call(kernel, out_shape=(jax.ShapeDtypeStruct((N, N), F32), jax....  173 us
    unnamed x13, local copies, waits for them, and re-layouts  5.66 us

profile of v3, /device:TPU:32, one launch (start us, length us, event | category | flops | bytes accessed | tf_op | source)
XLA Modules:
  0.0 179.7 jit_solution(4161200498195501976)
XLA Ops:
  0.6 173.4 %shard_map.101 = (f32[512,512]{1,0:T(8,128)}, f32[512,512]{1,0:T(8,128)}, f32[5,32,512]{2,1,0:T(8,128)}, f32[32,256]{1,0:T(8,128)}, f32[16,512]{1,0:T(8,128)}) custom-call(f32[512,512]{1,0:T(8,128)} %x_ref.1, f32[512,512]{1,0:T(8,128)} %g_ref.1, s32[1,4]{1,0:T(1,128)} %bits_ref.1, f32[5,32,512]{2,1,0:T(8,128)} %bitcast.11, f32[32,256]{1,0:T(8,128)} %bitcast.12, ...), custom_call_target="tpu_custom_call" | custom-call | tf_op jit(solution)/shard_map/pallas_call | solution.py:645
  174.1 0.0 copy-start
  174.1 2.4 %copy.16 = f32[512,512]{1,0:T(8,128)} copy(f32[512,512]{1,0:T(8,128)} %get-tuple-element.20) | data formatting | bytes 2097152
  176.4 0.0 copy-done
  176.4 0.0 copy-start.1
  176.4 1.0 copy.17
  177.4 0.2 copy-done.1
  177.6 0.0 copy-start.3
  177.6 0.7 copy.18
  178.3 0.0 copy-done.3
  178.3 0.0 copy-start.2
  178.4 0.6 copy.19
  179.0 0.2 copy-done.2
  179.1 0.6 copy.20
Async XLA Ops:
  174.1 2.4 %copy-start = (f32[512,512]{1,0:T(8,128)S(1)}, f32[512,512]{1,0:T(8,128)}, u32[]{:S(2)}) copy-start(f32[512,512]{1,0:T(8,128)} %get-tuple-element.21) | copy-start | bytes 3145732
  176.4 1.2 copy-start.1
  177.6 0.8 copy-start.3
  178.3 0.8 copy-start.2

commit v4 on v3

--- a/solution.py
+++ b/solution.py
@@ -593,23 +593,23 @@
     sum_3(1)
     back_0(5)
     sum_2(3)
+    sum_2(5)
     sum_3(2)
     to_outputs(4)
-    sum_2(5)
     back_0(6)
+    to_outputs(2)
+    to_outputs(3)
+    add_8()
+    sum_4(0)
+    sum_4(4)
+    sum_4(1)
     sum_3(3)
-    to_outputs(2)
-    add_8()
     sum_3(5)
+    sum_4(2)
     back_0(7)
-    to_outputs(3)
-    sum_4(0)
-    sum_4(1)
-    sum_4(2)
     sum_4(3)
-    sum_4(4)
+    by_slot()
     sum_4(5)
-    by_slot()
 
     lr_drain()
     w_drain()

time: 180 us -> 180 us (level)
  no operation moved by 1% of the time
where the time goes in v4:
time: 180 us
  Pallas kernels  173 us (96%)
  local copies, waits for them, and re-layouts  5.66 us (3%)
    pallas_call x1, Pallas kernels, on_device(): pl.pallas_call(kernel, out_shape=(jax.ShapeDtypeStruct((N, N), F32), jax....  173 us
    unnamed x13, local copies, waits for them, and re-layouts  5.66 us

profile of v4, /device:TPU:32, one launch (start us, length us, event | category | flops | bytes accessed | tf_op | source)
XLA Modules:
  0.0 179.7 jit_solution(12929214352596816143)
XLA Ops:
  0.6 173.4 %shard_map.101 = (f32[512,512]{1,0:T(8,128)}, f32[512,512]{1,0:T(8,128)}, f32[5,32,512]{2,1,0:T(8,128)}, f32[32,256]{1,0:T(8,128)}, f32[16,512]{1,0:T(8,128)}) custom-call(f32[512,512]{1,0:T(8,128)} %x_ref.1, f32[512,512]{1,0:T(8,128)} %g_ref.1, s32[1,4]{1,0:T(1,128)} %bits_ref.1, f32[5,32,512]{2,1,0:T(8,128)} %bitcast.11, f32[32,256]{1,0:T(8,128)} %bitcast.12, ...), custom_call_target="tpu_custom_call" | custom-call | tf_op jit(solution)/shard_map/pallas_call | solution.py:645
  174.0 0.0 copy-start
  174.1 2.4 %copy.16 = f32[512,512]{1,0:T(8,128)} copy(f32[512,512]{1,0:T(8,128)} %get-tuple-element.20) | data formatting | bytes 2097152
  176.4 0.0 copy-done
  176.4 0.0 copy-start.1
  176.4 1.0 copy.17
  177.4 0.2 copy-done.1
  177.6 0.0 copy-start.3
  177.6 0.7 copy.18
  178.3 0.0 copy-done.3
  178.3 0.0 copy-start.2
  178.3 0.6 copy.19
  179.0 0.2 copy-done.2
  179.1 0.6 copy.20
Async XLA Ops:
  174.0 2.4 %copy-start = (f32[512,512]{1,0:T(8,128)S(1)}, f32[512,512]{1,0:T(8,128)}, u32[]{:S(2)}) copy-start(f32[512,512]{1,0:T(8,128)} %get-tuple-element.21) | copy-start | bytes 3145732
  176.4 1.2 copy-start.1
  177.6 0.8 copy-start.3
  178.3 0.8 copy-start.2
